TPU v7x, 32 devices: a whole 2x2x4 slice. The times are simulated.
32 devices in a mesh: dp: 16 (over z, y, x), tensor: 2 (over core).
Axes of the slice: x: 2, y: 2, z: 4, core: 2. Of those that a mesh axis runs over, the one named last changes fastest.
Arguments:
- tokens: bfloat16 [4096, 1024], P(('dp', 'tensor')), may hold values from -6 to 6
- cotangent: bfloat16 [4096, 1024], P(('dp', 'tensor')), may hold values from -6 to 6
- lengths: int32 [16], P('dp'), may hold values from 64 to 256, as said below
- w_query: bfloat16 [1024, 2048], P('dp', 'tensor'), may hold values from -0.1875 to 0.1875
- key_matrix: bfloat16 [1024, 1024], P('dp', 'tensor'), may hold values from -0.1875 to 0.1875
- value_matrix: bfloat16 [1024, 1024], P('dp', 'tensor'), may hold values from -0.1875 to 0.1875
- w_out: bfloat16 [1024, 2048], P('dp', 'tensor'), may hold values from -0.375 to 0.375
- w_gate: bfloat16 [1024, 3072], P('dp', 'tensor'), may hold values from -0.1875 to 0.1875
- w_up: bfloat16 [1024, 3072], P('dp', 'tensor'), may hold values from -0.1875 to 0.1875
- w_down: bfloat16 [1024, 3072], P('dp', 'tensor'), may hold values from -0.109375 to 0.109375
- gain_attn: float32 [1024], replicated, may hold values from 0.5 to 2
- gain_mlp: float32 [1024], replicated, may hold values from 0.5 to 2
- gain_query: float32 [128], replicated, may hold values from 0.5 to 2
- gain_key: float32 [128], replicated, may hold values from 0.5 to 2
Outputs:
- result: bfloat16 [4096, 1024], P(('dp', 'tensor'))
- grad_tokens: float32 [4096, 1024], P(('dp', 'tensor'))
- grad_w_query: float32 [1024, 2048], P('dp', 'tensor')
- grad_w_key: float32 [1024, 1024], P('dp', 'tensor')
- grad_w_value: float32 [1024, 1024], P('dp', 'tensor')
- grad_w_out: float32 [1024, 2048], P('dp', 'tensor')
- grad_w_gate: float32 [1024, 3072], P('dp', 'tensor')
- grad_w_up: float32 [1024, 3072], P('dp', 'tensor')
- grad_w_down: float32 [1024, 3072], P('dp', 'tensor')
- grad_gain_attn: float32 [1024], replicated
- grad_gain_mlp: float32 [1024], replicated
- grad_gain_query: float32 [128], replicated
- grad_gain_key: float32 [128], replicated
Inputs may be any that keep to these rules, and one draw needn't show every extreme that they name: `lengths`: some sequence fills all 256 token slots of its block.
All inputs are finite; a program needn't handle non-finite values.
Results may differ from a plain program's by a relative error of at most 0.013.
The roundings to bfloat16 on the way count: a program that leaves them out, or rounds other values in their place, can miss the bound.
Values may be sent and summed in bfloat16 or wider, within the bound.
A program may use at most 128 MiB of HBM per device.

v0:
```python
import jax
import jax.numpy as jnp
from jax import lax
from jax.sharding import PartitionSpec as P

QUERY_HEADS = 16
KEY_VALUE_HEADS = 8
HEAD_SIZE = 128


norm_eps = 1e-06
rope_base = 1000000.0


def rms_rows(values, gain_vec):
    inverse = lax.rsqrt(jnp.mean(values * values, axis=-1, keepdims=True) + norm_eps)
    return (values * inverse * gain_vec, inverse)


def rms_back(grad_output, values, inverse, gain_vec):
    scaled = grad_output * gain_vec
    mean_term = jnp.mean(scaled * values, axis=-1, keepdims=True)
    grad_values = inverse * scaled - values * (inverse * inverse * inverse) * mean_term
    flat_terms = (grad_output * values * inverse).reshape(-1, values.shape[-1])
    return (grad_values, jnp.sum(flat_terms, axis=0))


def layout(length_value, total_rows):
    length_value = jnp.asarray(length_value)
    indices = jnp.arange(total_rows, dtype=jnp.int32)
    live = indices < length_value
    positions = jnp.where(live, indices, jnp.zeros_like(indices))
    causal = live[:, None] & live[None, :] & (indices[None, :] <= indices[:, None])
    allowed = causal | (indices[:, None] == indices[None, :])
    return (positions, allowed)


def rope_tables(positions, head_width):
    half_width = head_width // 2
    frequency = jnp.exp(
        -jnp.log(rope_base) * (2.0 * jnp.arange(half_width, dtype=jnp.float32) / head_width)
    )
    angles = positions.astype(jnp.float32)[:, None] * frequency[None, :]
    return (jnp.cos(angles), jnp.sin(angles))


def rotate(values, cosine, sine_part):
    half_width = values.shape[-1] // 2
    first, second = (values[..., :half_width], values[..., half_width:])
    return jnp.concatenate(
        [first * cosine - second * sine_part, second * cosine + first * sine_part], axis=-1
    )


def rotate_back(grads, cosine, sine_part):
    half_width = grads.shape[-1] // 2
    first, second = (grads[..., :half_width], grads[..., half_width:])
    return jnp.concatenate(
        [first * cosine + second * sine_part, second * cosine - first * sine_part], axis=-1
    )


def product_t(left, right):
    return lax.dot_general(
        left, right, (((1,), (1,)), ((), ())), preferred_element_type=jnp.float32
    )


def product_tn(left, right):
    return lax.dot_general(
        left, right, (((0,), (0,)), ((), ())), preferred_element_type=jnp.float32
    )


def gather_rows(values):
    return lax.all_gather(values, "tensor", axis=0, tiled=True)


def scatter_rows(partial_sum):
    return lax.psum_scatter(partial_sum, "tensor", scatter_dimension=0, tiled=True)


def masked_scores(query_rot, key_rot, allowed, scaling):
    scores = (
        jnp.einsum("qgrd,kgd->grqk", query_rot, key_rot, preferred_element_type=jnp.float32)
        * scaling
    )
    return jnp.where(allowed, scores, -1e30)


def per_device(
    tokens,
    cotangent,
    lengths,
    w_query,
    key_matrix,
    value_matrix,
    w_out,
    w_gate,
    w_up,
    w_down,
    gain_attn,
    gain_mlp,
    gain_query,
    gain_key,
):
    own_rows = tokens.shape[0]
    total_rows = own_rows * lax.axis_size("tensor")
    length_value = lengths[0]
    positions, allowed = layout(length_value, total_rows)
    own_index = lax.axis_index("tensor") * own_rows + jnp.arange(own_rows, dtype=jnp.int32)
    own_live = own_index < length_value
    cot_live = jnp.where(own_live[:, None], cotangent, jnp.zeros_like(cotangent))
    cosine, sine_part = rope_tables(positions, HEAD_SIZE)
    cos_query, sin_query = (cosine[:, None, None, :], sine_part[:, None, None, :])
    cos_key, sin_key = (cosine[:, None, :], sine_part[:, None, :])
    scaling = HEAD_SIZE ** (-0.5)
    group_ratio = QUERY_HEADS // KEY_VALUE_HEADS
    token_values = tokens.astype(jnp.float32)
    attn_norm, attn_inverse = rms_rows(token_values, gain_attn)
    normed = gather_rows(attn_norm.astype(jnp.bfloat16))
    fetched = (
        lax.all_gather(w_query, "dp", axis=0, tiled=True),
        lax.all_gather(key_matrix, "dp", axis=0, tiled=True),
        lax.all_gather(value_matrix, "dp", axis=0, tiled=True),
        lax.all_gather(w_out, "dp", axis=0, tiled=True),
        lax.all_gather(w_gate, "dp", axis=0, tiled=True),
        lax.all_gather(w_up, "dp", axis=0, tiled=True),
        lax.all_gather(w_down, "dp", axis=0, tiled=True),
    )
    full_query, full_key, full_value, full_out, full_gate, full_up, full_down = fetched
    kv_heads = full_key.shape[1] // HEAD_SIZE
    query_raw = jnp.dot(normed, full_query, preferred_element_type=jnp.float32).reshape(
        total_rows, kv_heads, group_ratio, HEAD_SIZE
    )
    key_raw = jnp.dot(normed, full_key, preferred_element_type=jnp.float32).reshape(
        total_rows, kv_heads, HEAD_SIZE
    )
    value_part = (
        jnp.dot(normed, full_value, preferred_element_type=jnp.float32)
        .astype(jnp.bfloat16)
        .reshape(total_rows, kv_heads, HEAD_SIZE)
    )
    query_normed, query_inverse = rms_rows(query_raw, gain_query)
    key_normed, key_inverse = rms_rows(key_raw, gain_key)
    query_rot = rotate(query_normed, cos_query, sin_query).astype(jnp.bfloat16)
    key_rot = rotate(key_normed, cos_key, sin_key).astype(jnp.bfloat16)
    scores = masked_scores(query_rot, key_rot, allowed, scaling)
    row_max = jnp.max(scores, axis=-1, keepdims=True)
    log_total = row_max + jnp.log(jnp.sum(jnp.exp(scores - row_max), axis=-1, keepdims=True))
    attn_probs = jnp.exp(scores - log_total).astype(jnp.bfloat16)
    mixed = jnp.einsum(
        "grqk,kgd->qgrd", attn_probs, value_part, preferred_element_type=jnp.float32
    ).astype(jnp.bfloat16)
    mixed_flat = mixed.reshape(total_rows, -1)
    resid = token_values + scatter_rows(product_t(mixed_flat, full_out))
    mlp_norm, mlp_inverse = rms_rows(resid, gain_mlp)
    mlp_in = gather_rows(mlp_norm.astype(jnp.bfloat16))
    gate_proj = jnp.dot(mlp_in, full_gate, preferred_element_type=jnp.float32)
    up_proj = jnp.dot(mlp_in, full_up, preferred_element_type=jnp.float32)
    activation = (jax.nn.silu(gate_proj) * up_proj).astype(jnp.bfloat16)
    result = (resid + scatter_rows(product_t(activation, full_down))).astype(jnp.bfloat16)
    refetched = (
        lax.all_gather(w_query, "dp", axis=0, tiled=True),
        lax.all_gather(key_matrix, "dp", axis=0, tiled=True),
        lax.all_gather(value_matrix, "dp", axis=0, tiled=True),
        lax.all_gather(w_out, "dp", axis=0, tiled=True),
        lax.all_gather(w_gate, "dp", axis=0, tiled=True),
        lax.all_gather(w_up, "dp", axis=0, tiled=True),
        lax.all_gather(w_down, "dp", axis=0, tiled=True),
    )
    full_query, full_key, full_value, full_out, full_gate, full_up, full_down = refetched
    grad_result = gather_rows(cot_live)
    grad_w_down = product_tn(grad_result, activation)
    grad_act = jnp.dot(grad_result, full_down, preferred_element_type=jnp.float32)
    sigma = jax.nn.sigmoid(gate_proj)
    grad_gate = (grad_act * up_proj * sigma * (1.0 + gate_proj * (1.0 - sigma))).astype(
        jnp.bfloat16
    )
    grad_up = (grad_act * gate_proj * sigma).astype(jnp.bfloat16)
    grad_w_gate = product_tn(mlp_in, grad_gate)
    grad_w_up = product_tn(mlp_in, grad_up)
    grad_mlp_in = scatter_rows(product_t(grad_gate, full_gate) + product_t(grad_up, full_up))
    grad_resid_mlp, grad_gain_mlp = rms_back(grad_mlp_in, resid, mlp_inverse, gain_mlp)
    grad_resid = cot_live.astype(jnp.float32) + grad_resid_mlp
    grad_attn = gather_rows(grad_resid.astype(jnp.bfloat16))
    grad_w_out = product_tn(grad_attn, mixed_flat)
    grad_mixed = (
        jnp.dot(grad_attn, full_out, preferred_element_type=jnp.float32)
        .astype(jnp.bfloat16)
        .reshape(total_rows, kv_heads, group_ratio, HEAD_SIZE)
    )
    scores = masked_scores(query_rot, key_rot, allowed, scaling)
    probs_full = jnp.exp(scores - log_total)
    probs_half = probs_full.astype(jnp.bfloat16)
    grad_value = jnp.einsum(
        "grqk,qgrd->kgd", probs_half, grad_mixed, preferred_element_type=jnp.float32
    )
    grad_probs = jnp.einsum(
        "qgrd,kgd->grqk", grad_mixed, value_part, preferred_element_type=jnp.float32
    )
    row_delta = jnp.sum(grad_mixed.astype(jnp.float32) * mixed.astype(jnp.float32), axis=-1)
    row_delta = jnp.transpose(row_delta, (1, 2, 0))[..., None]
    grad_scores = (probs_full * (grad_probs - row_delta) * scaling).astype(jnp.bfloat16)
    grad_query_rot = jnp.einsum(
        "grqk,kgd->qgrd", grad_scores, key_rot, preferred_element_type=jnp.float32
    )
    grad_key_rot = jnp.einsum(
        "grqk,qgrd->kgd", grad_scores, query_rot, preferred_element_type=jnp.float32
    )
    grad_query_raw, grad_gain_query = rms_back(
        rotate_back(grad_query_rot, cos_query, sin_query), query_raw, query_inverse, gain_query
    )
    grad_key_raw, grad_gain_key = rms_back(
        rotate_back(grad_key_rot, cos_key, sin_key), key_raw, key_inverse, gain_key
    )
    grad_query_half = grad_query_raw.astype(jnp.bfloat16).reshape(total_rows, -1)
    grad_key_half = grad_key_raw.astype(jnp.bfloat16).reshape(total_rows, -1)
    grad_value_half = grad_value.astype(jnp.bfloat16).reshape(total_rows, -1)
    grad_w_query = product_tn(normed, grad_query_half)
    grad_w_key = product_tn(normed, grad_key_half)
    grad_w_value = product_tn(normed, grad_value_half)
    normed_terms = product_t(grad_query_half, full_query) + product_t(grad_key_half, full_key)
    normed_terms = normed_terms + product_t(grad_value_half, full_value)
    grad_normed = scatter_rows(normed_terms)
    grad_tokens_attn, grad_gain_attn = rms_back(grad_normed, token_values, attn_inverse, gain_attn)
    grad_tokens = grad_resid + grad_tokens_attn
    weight_sums = (
        lax.psum_scatter(grad_w_query, "dp", scatter_dimension=0, tiled=True),
        lax.psum_scatter(grad_w_key, "dp", scatter_dimension=0, tiled=True),
        lax.psum_scatter(grad_w_value, "dp", scatter_dimension=0, tiled=True),
        lax.psum_scatter(grad_w_out, "dp", scatter_dimension=0, tiled=True),
        lax.psum_scatter(grad_w_gate, "dp", scatter_dimension=0, tiled=True),
        lax.psum_scatter(grad_w_up, "dp", scatter_dimension=0, tiled=True),
        lax.psum_scatter(grad_w_down, "dp", scatter_dimension=0, tiled=True),
    )
    gain_totals = lax.psum(
        (grad_gain_attn, grad_gain_mlp, grad_gain_query, grad_gain_key), ("dp", "tensor")
    )
    return (
        result,
        grad_tokens,
        weight_sums[0],
        weight_sums[1],
        weight_sums[2],
        weight_sums[3],
        weight_sums[4],
        weight_sums[5],
        weight_sums[6],
        gain_totals[0],
        gain_totals[1],
        gain_totals[2],
        gain_totals[3],
    )


def solution(mesh):
    in_specs = (
        P(("dp", "tensor"), None),
        P(("dp", "tensor"), None),
        P("dp"),
        P("dp", "tensor"),
        P("dp", "tensor"),
        P("dp", "tensor"),
        P("dp", "tensor"),
        P("dp", "tensor"),
        P("dp", "tensor"),
        P("dp", "tensor"),
        P(),
        P(),
        P(),
        P(),
    )
    out_specs = (
        P(("dp", "tensor"), None),
        P(("dp", "tensor"), None),
        P("dp", "tensor"),
        P("dp", "tensor"),
        P("dp", "tensor"),
        P("dp", "tensor"),
        P("dp", "tensor"),
        P("dp", "tensor"),
        P("dp", "tensor"),
        P(),
        P(),
        P(),
        P(),
    )
    return jax.shard_map(
        per_device, mesh=mesh, in_specs=in_specs, out_specs=out_specs, check_vma=False
    )
```

profile of v0, /device:TPU:0, one launch (start us, length us, event | category | flops | bytes accessed | tf_op | source)
XLA Modules:
  0.0 1377.1 jit_solution(10447580998256225647)
XLA Ops:
  17.0 51.6 %all-gather.10.cloned.1.call-done = bf16[1024,512]{1,0:T(8,128)(2,1)} async-done(((bf16[64,512]{1,0:T(8,128)(2,1)}), bf16[1024,512]{1,0:T(8,128)(2,1)}) %all-gather.10.cloned.1.call-update) | async-done | bytes 1048592 | tf_op jit(solution)/shard_map/all_gather | solution.py:124
  70.9 54.4 %all-gather.8.cloned.1.call-done = bf16[1024,512]{1,0:T(8,128)(2,1)} async-done(((bf16[64,512]{1,0:T(8,128)(2,1)}), bf16[1024,512]{1,0:T(8,128)(2,1)}) %all-gather.8.cloned.1.call-update) | async-done | bytes 1048592 | tf_op jit(solution)/shard_map/all_gather | solution.py:125
  129.6 57.7 %all-gather.12.cloned.1.call-done = bf16[1024,1024]{1,0:T(8,128)(2,1)} async-done(((bf16[64,1024]{1,0:T(8,128)(2,1)}), bf16[1024,1024]{1,0:T(8,128)(2,1)}) %all-gather.12.cloned.1.call-update) | async-done | bytes 2097168 | tf_op jit(solution)/shard_map/all_gather | solution.py:123
  198.6 50.5 %all-gather.14.cloned.1.call-done = bf16[1024,1024]{1,0:T(8,128)(2,1)} async-done(((bf16[64,1024]{1,0:T(8,128)(2,1)}), bf16[1024,1024]{1,0:T(8,128)(2,1)}) %all-gather.14.cloned.1.call-update) | async-done | bytes 2097168 | tf_op jit(solution)/shard_map/all_gather | solution.py:126
  265.3 66.5 %all-gather.16.cloned.1.call-done = bf16[1024,1536]{1,0:T(8,128)(2,1)} async-done(((bf16[64,1536]{1,0:T(8,128)(2,1)}), bf16[1024,1536]{1,0:T(8,128)(2,1)}) %all-gather.16.cloned.1.call-update) | async-done | bytes 3145744 | tf_op jit(solution)/shard_map/all_gather | solution.py:127
  331.8 4.2 fusion.37
  336.0 65.0 %all-gather.18.cloned.1.call-done = bf16[1024,1536]{1,0:T(8,128)(2,1)} async-done(((bf16[64,1536]{1,0:T(8,128)(2,1)}), bf16[1024,1536]{1,0:T(8,128)(2,1)}) %all-gather.18.cloned.1.call-update) | async-done | bytes 3145744 | tf_op jit(solution)/shard_map/all_gather | solution.py:128
  401.0 4.2 fusion.38
  405.2 65.0 %all-gather.20.cloned.1.call-done = bf16[1024,1536]{1,0:T(8,128)(2,1)} async-done(((bf16[64,1536]{1,0:T(8,128)(2,1)}), bf16[1024,1536]{1,0:T(8,128)(2,1)}) %all-gather.20.cloned.1.call-update) | async-done | bytes 3145744 | tf_op jit(solution)/shard_map/all_gather | solution.py:129
  470.2 5.4 multiply_convert_fusion
  480.2 4.1 fusion.39
  554.1 3.9 fusion.42
  559.0 3.9 fusion.45
  563.9 4.8 fusion.46
  568.8 4.8 fusion.47
  574.7 4.7 fusion.48
  588.9 40.3 %all-reduce = (f32[1024]{0:T(1024)}, f32[1024]{0:T(1024)}, f32[128]{0:T(128)}, f32[128]{0:T(128)}) all-reduce(f32[1024]{0:T(1024)S(1)} %get-tuple-element.15, f32[1024]{0:T(1024)S(1)} %get-tuple-element.13, f32[128]{0:T(128)S(1)} %fusion.6, f32[128]{0:T(128)S(1)} %fusion.21), channel_id=1, replica_groups=mesh['dp'=16,'tensor'=2] {'dp','tensor'}, use_global_device_ids=true, to_apply=%region_23.24 | all-reduce | flops 2304 | bytes 18432 | tf_op jit(solution)/shard_map/psum | solution.py:237
  631.2 9.7 reduce-scatter.22.cloned.1.call-done
  640.9 81.0 %reduce-scatter.24.cloned.1.call-done = f32[64,512]{1,0:T(8,128)} async-done(((f32[1024,512]{1,0:T(8,128)}), f32[64,512]{1,0:T(8,128)}) %reduce-scatter.24.cloned.1.call-update) | async-done | bytes 131088 | tf_op jit(solution)/shard_map/reduce_scatter | solution.py:231
  721.9 94.5 %reduce-scatter.20.cloned.1.call-done = f32[64,1024]{1,0:T(8,128)} async-done(((f32[1024,1024]{1,0:T(8,128)}), f32[64,1024]{1,0:T(8,128)}) %reduce-scatter.20.cloned.1.call-update) | async-done | bytes 262160 | tf_op jit(solution)/shard_map/reduce_scatter | solution.py:229
  816.4 97.5 %reduce-scatter.26.cloned.1.call-done = f32[64,1024]{1,0:T(8,128)} async-done(((f32[1024,1024]{1,0:T(8,128)}), f32[64,1024]{1,0:T(8,128)}) %reduce-scatter.26.cloned.1.call-update) | async-done | bytes 262160 | tf_op jit(solution)/shard_map/reduce_scatter | solution.py:232
  913.9 152.2 %reduce-scatter.28.cloned.1.call-done = f32[64,1536]{1,0:T(8,128)} async-done(((f32[1024,1536]{1,0:T(8,128)}), f32[64,1536]{1,0:T(8,128)}) %reduce-scatter.28.cloned.1.call-update) | async-done | bytes 393232 | tf_op jit(solution)/shard_map/reduce_scatter | solution.py:233
  1066.2 151.9 %reduce-scatter.30.cloned.1.call-done = f32[64,1536]{1,0:T(8,128)} async-done(((f32[1024,1536]{1,0:T(8,128)}), f32[64,1536]{1,0:T(8,128)}) %reduce-scatter.30.cloned.1.call-update) | async-done | bytes 393232 | tf_op jit(solution)/shard_map/reduce_scatter | solution.py:234
  1218.1 151.8 %reduce-scatter.32.cloned.1.call-done = f32[64,1536]{1,0:T(8,128)} async-done(((f32[1024,1536]{1,0:T(8,128)}), f32[64,1536]{1,0:T(8,128)}) %reduce-scatter.32.cloned.1.call-update) | async-done | bytes 393232 | tf_op jit(solution)/shard_map/reduce_scatter | solution.py:235
  (258 shorter events, 131.3 us)
Async XLA Ops:
  7.2 61.4 %all-gather.10.cloned.1.call-start = ((), (), s32[]{:S(2)}) async-start(), calls=%async_computation.12 | async-start | bytes 1114112 | tf_op jit(solution)/shard_map/all_gather | solution.py:124
  7.9 117.4 %all-gather.8.cloned.1.call-start = ((), (), s32[]{:S(2)}) async-start(), calls=%async_computation.11 | async-start | bytes 1114112 | tf_op jit(solution)/shard_map/all_gather | solution.py:125
  8.7 178.7 %all-gather.12.cloned.1.call-start = ((), (), s32[]{:S(2)}) async-start(), calls=%async_computation.13 | async-start | bytes 2228224 | tf_op jit(solution)/shard_map/all_gather | solution.py:123
  9.4 239.8 %all-gather.14.cloned.1.call-start = ((), (), s32[]{:S(2)}) async-start(), calls=%async_computation.14 | async-start | bytes 2228224 | tf_op jit(solution)/shard_map/all_gather | solution.py:126
  10.0 250.1 %reduce-scatter.12.cloned.1.call-start = ((), (), s32[]{:S(2)}) async-start(), calls=%async_computation.15 | async-start | bytes 1572864 | tf_op jit(solution)/shard_map/reduce_scatter | solution.py:80
  16.2 178.9 %copy-start.27 = (f32[256,64]{1,0:T(8,128)}, f32[256,64]{1,0:T(8,128)S(1)}, u32[]{:S(2)}) copy-start(f32[256,64]{1,0:T(8,128)S(1)} %get-tuple-element.46) | copy-start | bytes 196612
  70.2 58.1 %copy-start.53 = (f32[128]{0:T(128)S(1)}, f32[128]{0:T(128)}, u32[]{:S(2)}) copy-start(f32[128]{0:T(128)} %param.27) | copy-start | bytes 1540
  128.3 61.3 %copy-start.50 = (f32[256,4]{0,1:T(4,128)}, f32[256,4]{0,1:T(4,128)S(1)}, u32[]{:S(2)}) copy-start(f32[256,4]{0,1:T(4,128)S(1)} %get-tuple-element.44) | copy-start | bytes 12292
  252.7 79.1 %all-gather.16.cloned.1.call-start = ((), (), s32[]{:S(2)}) async-start(), calls=%async_computation.16 | async-start | bytes 3342336 | tf_op jit(solution)/shard_map/all_gather | solution.py:127
  253.3 147.7 %all-gather.18.cloned.1.call-start = ((), (), s32[]{:S(2)}) async-start(), calls=%async_computation.17 | async-start | bytes 3342336 | tf_op jit(solution)/shard_map/all_gather | solution.py:128
  254.0 216.2 %all-gather.20.cloned.1.call-start = ((), (), s32[]{:S(2)}) async-start(), calls=%async_computation.18 | async-start | bytes 3342336 | tf_op jit(solution)/shard_map/all_gather | solution.py:129
  254.8 248.6 %reduce-scatter.16.cloned.1.call-start = ((), (), s32[]{:S(2)}) async-start(), calls=%async_computation.20 | async-start | bytes 1572864 | tf_op jit(solution)/shard_map/reduce_scatter | solution.py:80
  480.1 25.2 %reduce-scatter.14.cloned.1.call-start = ((), (), s32[]{:S(2)}) async-start(), calls=%async_computation.19 | async-start | bytes 1572864 | tf_op jit(solution)/shard_map/reduce_scatter | solution.py:80
  484.3 103.3 %reduce-scatter.18.cloned.1.call-start = ((), (), s32[]{:S(2)}) async-start(), calls=%async_computation.21 | async-start | bytes 1572864 | tf_op jit(solution)/shard_map/reduce_scatter | solution.py:80
  495.6 7.8 copy-start.48
  548.1 92.9 %reduce-scatter.22.cloned.1.call-start = ((), (), s32[]{:S(2)}) async-start(), calls=%async_computation.23 | async-start | bytes 2228224 | tf_op jit(solution)/shard_map/reduce_scatter | solution.py:230
  551.0 170.9 %reduce-scatter.24.cloned.1.call-start = ((), (), s32[]{:S(2)}) async-start(), calls=%async_computation.24 | async-start | bytes 2228224 | tf_op jit(solution)/shard_map/reduce_scatter | solution.py:231
  553.8 262.6 %reduce-scatter.20.cloned.1.call-start = ((), (), s32[]{:S(2)}) async-start(), calls=%async_computation.22 | async-start | bytes 4456448 | tf_op jit(solution)/shard_map/reduce_scatter | solution.py:229
  558.0 355.9 %reduce-scatter.26.cloned.1.call-start = ((), (), s32[]{:S(2)}) async-start(), calls=%async_computation.25 | async-start | bytes 4456448 | tf_op jit(solution)/shard_map/reduce_scatter | solution.py:232
  562.9 503.3 %reduce-scatter.28.cloned.1.call-start = ((), (), s32[]{:S(2)}) async-start(), calls=%async_computation.26 | async-start | bytes 6684672 | tf_op jit(solution)/shard_map/reduce_scatter | solution.py:233
  568.8 649.3 %reduce-scatter.30.cloned.1.call-start = ((), (), s32[]{:S(2)}) async-start(), calls=%async_computation.27 | async-start | bytes 6684672 | tf_op jit(solution)/shard_map/reduce_scatter | solution.py:234
  573.7 796.2 %reduce-scatter.32.cloned.1.call-start = ((), (), s32[]{:S(2)}) async-start(), calls=%async_computation.28 | async-start | bytes 6684672 | tf_op jit(solution)/shard_map/reduce_scatter | solution.py:235
  586.9 42.3 %copy-start.42 = (f32[128,1024]{1,0:T(8,128)S(1)}, f32[128,1024]{1,0:T(8,128)}, u32[]{:S(2)}) copy-start(f32[128,1024]{1,0:T(8,128)} %get-tuple-element.24) | copy-start | bytes 1572868
  586.9 42.3 %copy-start.60 = (f32[128]{0:T(128)S(1)}, f32[128]{0:T(128)}, u32[]{:S(2)}) copy-start(f32[128]{0:T(128)} %get-tuple-element.47) | copy-start | bytes 1540
  (55 other events, 125.7 us)
Sparse Core Ops, SparseCore 0:
  10.7 57.7 all-gather.9
  71.3 53.9 all-gather.7
  128.1 59.2 all-gather.11
  190.0 59.1 all-gather.13
  252.8 7.1 reduce-scatter.11
  262.7 69.0 all-gather.15
  334.6 66.3 all-gather.17
  403.8 66.3 all-gather.19
  480.2 6.9 reduce-scatter.15
  489.3 9.5 reduce-scatter.13
  548.2 6.9 reduce-scatter.17
  557.9 83.0 reduce-scatter.21
  643.8 78.0 reduce-scatter.23
  724.6 91.7 reduce-scatter.19
  819.2 94.7 reduce-scatter.25
  919.6 146.5 reduce-scatter.27
  1071.8 146.1 reduce-scatter.29
  1223.7 146.0 reduce-scatter.31
where the time goes:
time: 1390 us; the launch traced here: 1380 us
  waiting for transfers between devices  1160 us (83%)
  matrix products  68.2 us (5%)
  local copies, waits for them, and re-layouts  54.8 us (4%)
  blocking collectives  49.9 us (4%)
  other arithmetic  31.9 us (2%)
  between operations  16.2 us (1%)
    reduce_scatter x1, waiting for transfers between devices, per_device(): lax.psum_scatter(grad_w_gate, 'dp', scatter_dimension=0, tiled=True)  152 us
    reduce_scatter x1, waiting for transfers between devices, per_device(): lax.psum_scatter(grad_w_up, 'dp', scatter_dimension=0, tiled=True)  152 us
    reduce_scatter x1, waiting for transfers between devices, per_device(): lax.psum_scatter(grad_w_down, 'dp', scatter_dimension=0, tiled=True)  152 us
    reduce_scatter x1, waiting for transfers between devices, per_device(): lax.psum_scatter(grad_w_out, 'dp', scatter_dimension=0, tiled=True)  97.5 us
    reduce_scatter x1, waiting for transfers between devices, per_device(): lax.psum_scatter(grad_w_query, 'dp', scatter_dimension=0, tiled=True)  94.5 us
    reduce_scatter x1, waiting for transfers between devices, per_device(): lax.psum_scatter(grad_w_value, 'dp', scatter_dimension=0, tiled=True)  81 us
    all_gather x1, waiting for transfers between devices, per_device(): lax.all_gather(w_gate, 'dp', axis=0, tiled=True)  66.5 us
    all_gather x1, waiting for transfers between devices, per_device(): lax.all_gather(w_down, 'dp', axis=0, tiled=True)  65 us
  transfers between devices with their start and end apart: 18, of which 15 were waited for; matrix products, arithmetic and copies ran while one was open for 7% of the time, Pallas kernels for 0%

commit v1 on v0

--- a/solution.py
+++ b/solution.py
@@ -1,7 +1,15 @@
+import functools
+import math
+
 import jax
 import jax.numpy as jnp
 from jax import lax
+from jax.experimental import pallas as pl
+from jax.experimental.pallas import tpu as pltpu
 from jax.sharding import PartitionSpec as P
+
+MESH = pl.DeviceIdType.MESH
+VMEM_LIMIT = 64000000
 
 QUERY_HEADS = 16
 KEY_VALUE_HEADS = 8
@@ -72,12 +80,481 @@
     )
 
 
-def gather_rows(values):
-    return lax.all_gather(values, "tensor", axis=0, tiled=True)
-
-
-def scatter_rows(partial_sum):
-    return lax.psum_scatter(partial_sum, "tensor", scatter_dimension=0, tiled=True)
+def split_dims(count):
+    sizes, rest = [], count
+    for _ in range(2):
+        if rest % 2 == 0:
+            sizes.append(2)
+            rest //= 2
+    while rest > 1:
+        factor = 4 if rest % 4 == 0 else rest
+        sizes.insert(0, factor)
+        rest //= factor
+    return tuple(sizes)
+
+
+def dim_orders(sizes):
+    k = len(sizes)
+    base = list(range(k))
+    if k < 2:
+        return [tuple(base)]
+    swapped = base[:-2] + [base[-1], base[-2]]
+    if k < 3:
+        return [tuple(base), tuple(swapped)]
+    late = [k - 2] + base[: k - 2] + [k - 1]
+    late_swapped = [k - 1] + base[: k - 2] + [k - 2]
+    return [tuple(base), tuple(swapped), tuple(base), tuple(swapped), tuple(late), tuple(late_swapped)]
+
+
+def plan_chunks(widths, sizes):
+    orders = dim_orders(sizes)
+    chunks = []
+    for index, width in enumerate(widths):
+        parts = 2 if width % 256 == 0 else 1
+        for part in range(parts):
+            step = width // parts
+            chunks.append((index, part * step, step, orders[len(chunks) % len(orders)]))
+    return chunks
+
+
+class Place:
+    def __init__(self, sizes):
+        self.sizes = sizes
+        self.me = lax.axis_index("dp")
+        self.strides = [math.prod(sizes[i + 1 :]) for i in range(len(sizes))]
+        self.coords = [
+            lax.rem(lax.div(self.me, stride), size) for stride, size in zip(self.strides, sizes)
+        ]
+        self.base = [sum(size - 1 for size in sizes[:i]) for i in range(len(sizes))]
+
+    def other(self, dim, offset):
+        return lax.rem(self.coords[dim] + offset, self.sizes[dim])
+
+    def peer(self, dim, offset):
+        return self.me + (self.other(dim, offset) - self.coords[dim]) * self.strides[dim]
+
+    def slot(self, dim, offset):
+        return self.base[dim] + offset - 1
+
+    def barrier(self, extra=()):
+        barrier = pltpu.get_barrier_semaphore()
+        count = 0
+        for dim, size in enumerate(self.sizes):
+            for offset in range(1, size):
+                pl.semaphore_signal(
+                    barrier, inc=1, device_id={"dp": self.peer(dim, offset)}, device_id_type=MESH
+                )
+                count += 1
+        for target in extra:
+            pl.semaphore_signal(barrier, inc=1, device_id=target, device_id_type=MESH)
+            count += 1
+        pl.semaphore_wait(barrier, count)
+
+
+def gather_kernel(sizes, chunks, count, *refs):
+    ins, outs = refs[:count], refs[count : 2 * count]
+    send_sem, recv_sem, local_sem = refs[2 * count :]
+    place = Place(sizes)
+    k = len(sizes)
+
+    def region(chunk, done, dim=None, coord=None):
+        index, start, width, _ = chunk
+        where = []
+        for i in range(k):
+            if i == dim:
+                where.append(coord)
+            elif i in done:
+                where.append(slice(None))
+            else:
+                where.append(place.coords[i])
+        return outs[index].at[tuple(where) + (slice(None), pl.ds(start, width))]
+
+    def sends(j, stage):
+        chunk = chunks[j]
+        order = chunk[3]
+        dim, done = order[stage], order[:stage]
+        block = region(chunk, done)
+        if stage == 0:
+            source = ins[chunk[0]].at[:, pl.ds(chunk[1], chunk[2])]
+        else:
+            source = block
+        return [
+            pltpu.make_async_remote_copy(
+                src_ref=source,
+                dst_ref=block,
+                send_sem=send_sem.at[j, place.slot(dim, offset)],
+                recv_sem=recv_sem.at[j, place.slot(dim, offset)],
+                device_id={"dp": place.peer(dim, offset)},
+                device_id_type=MESH,
+            )
+            for offset in range(1, sizes[dim])
+        ]
+
+    def wait_arrivals(j, stage):
+        chunk = chunks[j]
+        order = chunk[3]
+        dim, done = order[stage], order[:stage]
+        for offset in range(1, sizes[dim]):
+            block = region(chunk, done, dim, place.other(dim, sizes[dim] - offset))
+            pltpu.make_async_remote_copy(
+                src_ref=block,
+                dst_ref=block,
+                send_sem=send_sem.at[j, place.slot(dim, offset)],
+                recv_sem=recv_sem.at[j, place.slot(dim, offset)],
+                device_id={"dp": place.peer(dim, offset)},
+                device_id_type=MESH,
+            ).wait_recv()
+
+    place.barrier()
+    started, own = [], []
+    for j, chunk in enumerate(chunks):
+        copies = sends(j, 0)
+        for copy in copies:
+            copy.start()
+        started += copies
+        copy = pltpu.make_async_copy(
+            ins[chunk[0]].at[:, pl.ds(chunk[1], chunk[2])], region(chunk, ()), local_sem.at[j]
+        )
+        copy.start()
+        own.append(copy)
+    for step in range(len(chunks) + k - 1):
+        for stage in range(1, k + 1):
+            j = step - (stage - 1)
+            if not 0 <= j < len(chunks):
+                continue
+            if stage == 1:
+                own[j].wait()
+            wait_arrivals(j, stage - 1)
+            if stage < k:
+                copies = sends(j, stage)
+                for copy in copies:
+                    copy.start()
+                started += copies
+    for copy in started:
+        copy.wait_send()
+
+
+def gather_weights(weights, collective_id):
+    sizes = split_dims(lax.axis_size("dp"))
+    chunks = plan_chunks([weight.shape[1] for weight in weights], sizes)
+    peers = sum(size - 1 for size in sizes)
+    count = len(weights)
+    outs = pl.pallas_call(
+        functools.partial(gather_kernel, sizes, chunks, count),
+        out_shape=[jax.ShapeDtypeStruct(sizes + w.shape, w.dtype) for w in weights],
+        in_specs=[pl.BlockSpec(memory_space=pltpu.VMEM)] * count,
+        out_specs=[pl.BlockSpec(memory_space=pl.ANY)] * count,
+        scratch_shapes=[
+            pltpu.SemaphoreType.DMA((len(chunks), peers)),
+            pltpu.SemaphoreType.DMA((len(chunks), peers)),
+            pltpu.SemaphoreType.DMA((len(chunks),)),
+        ],
+        compiler_params=pltpu.CompilerParams(
+            collective_id=collective_id, has_side_effects=True, vmem_limit_bytes=VMEM_LIMIT
+        ),
+    )(*weights)
+    return [out.reshape(-1, out.shape[-1]) for out in outs]
+
+
+def reduce_kernel(sizes, chunks, count, tensor_size, *refs):
+    ins, gains = refs[:count], refs[count]
+    outs, gain_out = refs[count + 1 : 2 * count + 1], refs[2 * count + 1]
+    rest = list(refs[2 * count + 2 :])
+    k = len(sizes)
+    held = [[rest.pop(0) for _ in range(k - 1)] for _ in chunks]
+    landed = [[rest.pop(0) for _ in range(k)] for _ in chunks]
+    gain_held = [rest.pop(0) for _ in range(k)]
+    gain_landed = [rest.pop(0) for _ in range(k + 1)]
+    send_sem, recv_sem, local_sem, gain_send, gain_recv = rest
+    place = Place(sizes)
+    tensor_me = lax.axis_index("tensor")
+    rows = ins[0].shape[-2]
+
+    def remote(source, target, send, recv, device):
+        return pltpu.make_async_remote_copy(
+            src_ref=source,
+            dst_ref=target,
+            send_sem=send,
+            recv_sem=recv,
+            device_id=device,
+            device_id_type=MESH,
+        )
+
+    def part(ref, dims, dim, coord, columns):
+        where = tuple(coord if i == dim else slice(None) for i in dims)
+        return ref.at[where + (slice(None), columns)]
+
+    def copies_of(j, stage):
+        index, start, width, order = chunks[j]
+        dim = order[stage]
+        dims = [i for i in range(k) if i not in order[:stage]]
+        if stage == 0:
+            ref, columns = ins[index], pl.ds(start, width)
+        else:
+            ref, columns = held[j][stage - 1], slice(None)
+        result = []
+        for offset in range(1, sizes[dim]):
+            source = part(ref, dims, dim, place.other(dim, offset), columns)
+            slot = place.slot(dim, offset)
+            result.append(
+                remote(
+                    source,
+                    landed[j][stage].at[offset - 1],
+                    send_sem.at[j, slot],
+                    recv_sem.at[j, slot],
+                    {"dp": place.peer(dim, offset)},
+                )
+            )
+        return result
+
+    def add_up(j, stage):
+        index, start, width, order = chunks[j]
+        dim = order[stage]
+        dims = [i for i in range(k) if i not in order[:stage]]
+        lead = [sizes[i] for i in dims if i != dim]
+        blocks = math.prod(lead)
+        per = rows // 16
+
+        def body(i, carry):
+            rows_at = pl.ds(pl.multiple_of(lax.rem(i, per) * 16, 16), 16)
+            flat = lax.div(i, per)
+            where = []
+            for position in range(len(lead)):
+                below = math.prod(lead[position + 1 :])
+                where.append(lax.rem(lax.div(flat, below), lead[position]))
+            if stage == 0:
+                own = tuple(where)
+                source = held[j][0]
+            else:
+                own = list(where)
+                own.insert(dims.index(dim), place.coords[dim])
+                own = tuple(own)
+                source = held[j][stage - 1]
+            total = source[own + (rows_at, slice(None))].astype(jnp.float32)
+            for offset in range(1, sizes[dim]):
+                got = landed[j][stage][(offset - 1,) + tuple(where) + (rows_at, slice(None))]
+                total = total + got.astype(jnp.float32)
+            if stage < k - 1:
+                held[j][stage][tuple(where) + (rows_at, slice(None))] = total.astype(jnp.bfloat16)
+            else:
+                outs[index][rows_at, pl.ds(start, width)] = total
+            return carry
+
+        lax.fori_loop(0, blocks * per, body, 0)
+
+    def gain_copies(stage):
+        source = gains if stage == 0 else gain_held[stage - 1]
+        result = []
+        if stage < k:
+            for offset in range(1, sizes[stage]):
+                slot = place.slot(stage, offset)
+                result.append(
+                    remote(
+                        source,
+                        gain_landed[stage].at[offset - 1],
+                        gain_send.at[slot],
+                        gain_recv.at[slot],
+                        {"dp": place.peer(stage, offset)},
+                    )
+                )
+        else:
+            first = sum(size - 1 for size in sizes)
+            for offset in range(1, tensor_size):
+                result.append(
+                    remote(
+                        source,
+                        gain_landed[stage].at[offset - 1],
+                        gain_send.at[first + offset - 1],
+                        gain_recv.at[first + offset - 1],
+                        {"tensor": lax.rem(tensor_me + offset, tensor_size)},
+                    )
+                )
+        return result
+
+    place.barrier(
+        [{"tensor": lax.rem(tensor_me + i, tensor_size)} for i in range(1, tensor_size)]
+    )
+    flights, own = [], []
+    for j, chunk in enumerate(chunks):
+        index, start, width, order = chunk
+        first = copies_of(j, 0)
+        for copy in first:
+            copy.start()
+        flights.append([first])
+        copy = pltpu.make_async_copy(
+            part(ins[index], range(k), order[0], place.coords[order[0]], pl.ds(start, width)),
+            held[j][0],
+            local_sem.at[j],
+        )
+        copy.start()
+        own.append(copy)
+        if j == 0:
+            gain_flight = gain_copies(0)
+            for copy in gain_flight:
+                copy.start()
+    for step in range(len(chunks) + k - 1):
+        if step <= k:
+            for copy in gain_flight:
+                copy.wait()
+            total = (gains if step == 0 else gain_held[step - 1])[...]
+            for i in range(len(gain_flight)):
+                total = total + gain_landed[step][i]
+            if step < k:
+                gain_held[step][...] = total
+                gain_flight = gain_copies(step + 1)
+                for copy in gain_flight:
+                    copy.start()
+            else:
+                gain_out[...] = total
+        for stage in range(k):
+            j = step - stage
+            if not 0 <= j < len(chunks):
+                continue
+            if stage == 0:
+                own[j].wait()
+            for copy in flights[j][stage]:
+                copy.wait_recv()
+            add_up(j, stage)
+            if stage < k - 1:
+                following = copies_of(j, stage + 1)
+                for copy in following:
+                    copy.start()
+                flights[j].append(following)
+    for flight in flights:
+        for copies in flight:
+            for copy in copies:
+                copy.wait_send()
+
+
+def reduce_weights(grads, gains, collective_id):
+    sizes = split_dims(lax.axis_size("dp"))
+    tensor_size = lax.axis_size("tensor")
+    k = len(sizes)
+    dp = math.prod(sizes)
+    rows = grads[0].shape[0] // dp
+    chunks = [
+        (index, start, width, tuple(reversed(order)))
+        for index, start, width, order in plan_chunks([g.shape[1] for g in grads], sizes)
+    ]
+    peers = sum(size - 1 for size in sizes)
+    count = len(grads)
+    held, landed = [], []
+    for _, _, width, order in chunks:
+        for stage in range(k):
+            left = tuple(sizes[i] for i in range(k) if i not in order[: stage + 1])
+            if stage < k - 1:
+                held.append(pltpu.VMEM(left + (rows, width), jnp.bfloat16))
+            landed.append(pltpu.VMEM((sizes[order[stage]] - 1,) + left + (rows, width), jnp.bfloat16))
+    gain_landed = [pltpu.VMEM((size - 1,) + gains.shape, jnp.float32) for size in sizes + (tensor_size,)]
+    whole = pl.BlockSpec(memory_space=pltpu.VMEM)
+    outs = pl.pallas_call(
+        functools.partial(reduce_kernel, sizes, chunks, count, tensor_size),
+        out_shape=[jax.ShapeDtypeStruct((rows, g.shape[1]), jnp.float32) for g in grads]
+        + [jax.ShapeDtypeStruct(gains.shape, jnp.float32)],
+        in_specs=[pl.BlockSpec(memory_space=pl.ANY)] * count + [whole],
+        out_specs=[whole] * (count + 1),
+        scratch_shapes=held
+        + landed
+        + [pltpu.VMEM(gains.shape, jnp.float32)] * k
+        + gain_landed
+        + [
+            pltpu.SemaphoreType.DMA((len(chunks), peers)),
+            pltpu.SemaphoreType.DMA((len(chunks), peers)),
+            pltpu.SemaphoreType.DMA((len(chunks),)),
+            pltpu.SemaphoreType.DMA((peers + tensor_size - 1,)),
+            pltpu.SemaphoreType.DMA((peers + tensor_size - 1,)),
+        ],
+        compiler_params=pltpu.CompilerParams(
+            collective_id=collective_id, has_side_effects=True, vmem_limit_bytes=VMEM_LIMIT
+        ),
+    )(*[g.reshape(sizes + (rows, g.shape[1])) for g in grads], gains)
+    return outs[:count], outs[count]
+
+
+def pair_barrier(size):
+    me = lax.axis_index("tensor")
+    barrier = pltpu.get_barrier_semaphore()
+    for offset in range(1, size):
+        pl.semaphore_signal(
+            barrier, inc=1, device_id={"tensor": lax.rem(me + offset, size)}, device_id_type=MESH
+        )
+    pl.semaphore_wait(barrier, size - 1)
+    return me
+
+
+def gather_rows_kernel(size, in_ref, out_ref, send_sem, recv_sem):
+    me = pair_barrier(size)
+    copies = []
+    for offset in range(1, size):
+        copy = pltpu.make_async_remote_copy(
+            src_ref=in_ref,
+            dst_ref=out_ref.at[me],
+            send_sem=send_sem.at[offset - 1],
+            recv_sem=recv_sem.at[offset - 1],
+            device_id={"tensor": lax.rem(me + offset, size)},
+            device_id_type=MESH,
+        )
+        copy.start()
+        copies.append(copy)
+    out_ref[me] = in_ref[...]
+    for copy in copies:
+        copy.wait()
+
+
+def gather_rows(values, collective_id):
+    size = lax.axis_size("tensor")
+    out = pl.pallas_call(
+        functools.partial(gather_rows_kernel, size),
+        out_shape=jax.ShapeDtypeStruct((size,) + values.shape, values.dtype),
+        in_specs=[pl.BlockSpec(memory_space=pltpu.VMEM)],
+        out_specs=pl.BlockSpec(memory_space=pltpu.VMEM),
+        scratch_shapes=[pltpu.SemaphoreType.DMA((size - 1,))] * 2,
+        compiler_params=pltpu.CompilerParams(collective_id=collective_id, has_side_effects=True),
+    )(values)
+    return out.reshape(-1, values.shape[-1])
+
+
+def scatter_rows_kernel(size, in_ref, out_ref, landed, send_sem, recv_sem):
+    me = pair_barrier(size)
+    copies = []
+    for offset in range(1, size):
+        other = lax.rem(me + offset, size)
+        copy = pltpu.make_async_remote_copy(
+            src_ref=in_ref.at[other],
+            dst_ref=landed.at[offset - 1],
+            send_sem=send_sem.at[offset - 1],
+            recv_sem=recv_sem.at[offset - 1],
+            device_id={"tensor": other},
+            device_id_type=MESH,
+        )
+        copy.start()
+        copies.append(copy)
+    for copy in copies:
+        copy.wait()
+
+    def body(i, carry):
+        at = pl.ds(pl.multiple_of(i * 16, 16), 16)
+        total = in_ref[me, at, :]
+        for offset in range(1, size):
+            total = total + landed[offset - 1, at, :]
+        out_ref[at, :] = total
+        return carry
+
+    lax.fori_loop(0, out_ref.shape[0] // 16, body, 0)
+
+
+def scatter_rows(partial_sum, collective_id):
+    size = lax.axis_size("tensor")
+    rows, width = partial_sum.shape[0] // size, partial_sum.shape[1]
+    return pl.pallas_call(
+        functools.partial(scatter_rows_kernel, size),
+        out_shape=jax.ShapeDtypeStruct((rows, width), partial_sum.dtype),
+        in_specs=[pl.BlockSpec(memory_space=pltpu.VMEM)],
+        out_specs=pl.BlockSpec(memory_space=pltpu.VMEM),
+        scratch_shapes=[pltpu.VMEM((size - 1, rows, width), partial_sum.dtype)]
+        + [pltpu.SemaphoreType.DMA((size - 1,))] * 2,
+        compiler_params=pltpu.CompilerParams(collective_id=collective_id, has_side_effects=True),
+    )(partial_sum.reshape(size, rows, width))
 
 
 def masked_scores(query_rot, key_rot, allowed, scaling):
@@ -118,15 +595,9 @@
     group_ratio = QUERY_HEADS // KEY_VALUE_HEADS
     token_values = tokens.astype(jnp.float32)
     attn_norm, attn_inverse = rms_rows(token_values, gain_attn)
-    normed = gather_rows(attn_norm.astype(jnp.bfloat16))
-    fetched = (
-        lax.all_gather(w_query, "dp", axis=0, tiled=True),
-        lax.all_gather(key_matrix, "dp", axis=0, tiled=True),
-        lax.all_gather(value_matrix, "dp", axis=0, tiled=True),
-        lax.all_gather(w_out, "dp", axis=0, tiled=True),
-        lax.all_gather(w_gate, "dp", axis=0, tiled=True),
-        lax.all_gather(w_up, "dp", axis=0, tiled=True),
-        lax.all_gather(w_down, "dp", axis=0, tiled=True),
+    normed = gather_rows(attn_norm.astype(jnp.bfloat16), 3)
+    fetched = gather_weights(
+        (w_query, key_matrix, value_matrix, w_out, w_gate, w_up, w_down), collective_id=0
     )
     full_query, full_key, full_value, full_out, full_gate, full_up, full_down = fetched
     kv_heads = full_key.shape[1] // HEAD_SIZE
@@ -153,24 +624,14 @@
         "grqk,kgd->qgrd", attn_probs, value_part, preferred_element_type=jnp.float32
     ).astype(jnp.bfloat16)
     mixed_flat = mixed.reshape(total_rows, -1)
-    resid = token_values + scatter_rows(product_t(mixed_flat, full_out))
+    resid = token_values + scatter_rows(product_t(mixed_flat, full_out), 7)
     mlp_norm, mlp_inverse = rms_rows(resid, gain_mlp)
-    mlp_in = gather_rows(mlp_norm.astype(jnp.bfloat16))
+    mlp_in = gather_rows(mlp_norm.astype(jnp.bfloat16), 4)
     gate_proj = jnp.dot(mlp_in, full_gate, preferred_element_type=jnp.float32)
     up_proj = jnp.dot(mlp_in, full_up, preferred_element_type=jnp.float32)
     activation = (jax.nn.silu(gate_proj) * up_proj).astype(jnp.bfloat16)
-    result = (resid + scatter_rows(product_t(activation, full_down))).astype(jnp.bfloat16)
-    refetched = (
-        lax.all_gather(w_query, "dp", axis=0, tiled=True),
-        lax.all_gather(key_matrix, "dp", axis=0, tiled=True),
-        lax.all_gather(value_matrix, "dp", axis=0, tiled=True),
-        lax.all_gather(w_out, "dp", axis=0, tiled=True),
-        lax.all_gather(w_gate, "dp", axis=0, tiled=True),
-        lax.all_gather(w_up, "dp", axis=0, tiled=True),
-        lax.all_gather(w_down, "dp", axis=0, tiled=True),
-    )
-    full_query, full_key, full_value, full_out, full_gate, full_up, full_down = refetched
-    grad_result = gather_rows(cot_live)
+    result = (resid + scatter_rows(product_t(activation, full_down), 8)).astype(jnp.bfloat16)
+    grad_result = gather_rows(cot_live, 5)
     grad_w_down = product_tn(grad_result, activation)
     grad_act = jnp.dot(grad_result, full_down, preferred_element_type=jnp.float32)
     sigma = jax.nn.sigmoid(gate_proj)
@@ -180,10 +641,10 @@
     grad_up = (grad_act * gate_proj * sigma).astype(jnp.bfloat16)
     grad_w_gate = product_tn(mlp_in, grad_gate)
     grad_w_up = product_tn(mlp_in, grad_up)
-    grad_mlp_in = scatter_rows(product_t(grad_gate, full_gate) + product_t(grad_up, full_up))
+    grad_mlp_in = scatter_rows(product_t(grad_gate, full_gate) + product_t(grad_up, full_up), 9)
     grad_resid_mlp, grad_gain_mlp = rms_back(grad_mlp_in, resid, mlp_inverse, gain_mlp)
     grad_resid = cot_live.astype(jnp.float32) + grad_resid_mlp
-    grad_attn = gather_rows(grad_resid.astype(jnp.bfloat16))
+    grad_attn = gather_rows(grad_resid.astype(jnp.bfloat16), 6)
     grad_w_out = product_tn(grad_attn, mixed_flat)
     grad_mixed = (
         jnp.dot(grad_attn, full_out, preferred_element_type=jnp.float32)
@@ -222,21 +683,34 @@
     grad_w_value = product_tn(normed, grad_value_half)
     normed_terms = product_t(grad_query_half, full_query) + product_t(grad_key_half, full_key)
     normed_terms = normed_terms + product_t(grad_value_half, full_value)
-    grad_normed = scatter_rows(normed_terms)
+    grad_normed = scatter_rows(normed_terms, 10)
     grad_tokens_attn, grad_gain_attn = rms_back(grad_normed, token_values, attn_inverse, gain_attn)
     grad_tokens = grad_resid + grad_tokens_attn
-    weight_sums = (
-        lax.psum_scatter(grad_w_query, "dp", scatter_dimension=0, tiled=True),
-        lax.psum_scatter(grad_w_key, "dp", scatter_dimension=0, tiled=True),
-        lax.psum_scatter(grad_w_value, "dp", scatter_dimension=0, tiled=True),
-        lax.psum_scatter(grad_w_out, "dp", scatter_dimension=0, tiled=True),
-        lax.psum_scatter(grad_w_gate, "dp", scatter_dimension=0, tiled=True),
-        lax.psum_scatter(grad_w_up, "dp", scatter_dimension=0, tiled=True),
-        lax.psum_scatter(grad_w_down, "dp", scatter_dimension=0, tiled=True),
-    )
-    gain_totals = lax.psum(
-        (grad_gain_attn, grad_gain_mlp, grad_gain_query, grad_gain_key), ("dp", "tensor")
-    )
+    gain_parts = (grad_gain_attn, grad_gain_mlp, grad_gain_query, grad_gain_key)
+    gain_rows = [part.reshape(-1, HEAD_SIZE) for part in gain_parts]
+    used = sum(part.shape[0] for part in gain_rows)
+    gain_rows.append(jnp.zeros((-used % 8, HEAD_SIZE), jnp.float32))
+    weight_sums, gain_sum = reduce_weights(
+        [
+            grad.astype(jnp.bfloat16)
+            for grad in (
+                grad_w_query,
+                grad_w_key,
+                grad_w_value,
+                grad_w_out,
+                grad_w_gate,
+                grad_w_up,
+                grad_w_down,
+            )
+        ],
+        jnp.concatenate(gain_rows, axis=0),
+        collective_id=1,
+    )
+    gain_totals, row = [], 0
+    for part in gain_parts:
+        taken = part.shape[0] // HEAD_SIZE
+        gain_totals.append(gain_sum[row : row + taken].reshape(-1))
+        row += taken
     return (
         result,
         grad_tokens,

time: 1390 us -> 525 us (0.38)
  waiting for transfers between devices: 1160 us -> 0 us
  Pallas kernels: 0 us -> 424 us
  blocking collectives: 49.9 us -> 0 us
  local copies, waits for them, and re-layouts: 54.8 us -> 25.6 us
  matrix products: 68.2 us -> 53.9 us
  between operations: 16.2 us -> 2 us
  other arithmetic: 31.9 us -> 17.9 us
    reduce_scatter x11 -> x0, waiting for transfers between devices: 740 us -> none  [the longest x1 152 us: per_device(): lax.psum_scatter(grad_w_gate, 'dp', scatter_dimension=0, tiled=True)]
    pallas_call x0 -> x10, Pallas kernels: none -> 424 us  [the longest x1 221 us: reduce_weights(): pl.pallas_call(functools.partial(reduce_kernel, sizes, chunks, count, ten...]
    all_gather x7 -> x0, waiting for transfers between devices: 411 us -> none  [the longest x1 66.5 us: per_device(): lax.all_gather(w_gate, 'dp', axis=0, tiled=True)]
    psum x1 -> x0, blocking collectives: 40.3 us -> none  [per_device(): lax.psum((grad_gain_attn, grad_gain_mlp, grad_gain_query, grad_gain_key),...]
    mul x13 -> x0, local copies, waits for them, and re-layouts: 24.6 us -> none  [the longest x6 13.8 us: rms_back(): values * (inverse * inverse * inverse) * mean_term]
  transfers between devices with their start and end apart: 18 -> 0, of which waited for: 15 -> 0; matrix products, arithmetic and copies ran while one was open for 7% -> 0% of each run, Pallas kernels for 0% -> 0%
where the time goes in v1:
time: 525 us; the launch traced here: 524 us
  Pallas kernels  424 us (81%)
  matrix products  53.9 us (10%)
  local copies, waits for them, and re-layouts  25.6 us (5%)
  other arithmetic  17.9 us (3%)
    pallas_call x1, Pallas kernels, reduce_weights(): pl.pallas_call(functools.partial(reduce_kernel, sizes, chunks, count, ten...  221 us
    pallas_call x1, Pallas kernels, gather_weights(): pl.pallas_call(functools.partial(gather_kernel, sizes, chunks, count), ou...  174 us
    pallas_call x4, Pallas kernels, scatter_rows(): pl.pallas_call(functools.partial(scatter_rows_kernel, size), out_shape=ja...  16.3 us
    dot_general x7, matrix products, product_tn(): lax.dot_general(left, right, (((0,), (0,)), ((), ())), preferred_element_...  15.2 us
    dot_general x7, matrix products, product_t(): lax.dot_general(left, right, (((1,), (1,)), ((), ())), preferred_element_...  13.5 us
    pallas_call x4, Pallas kernels, gather_rows(): pl.pallas_call(functools.partial(gather_rows_kernel, size), out_shape=jax...  13.1 us
    unnamed x131, local copies, waits for them, and re-layouts  12.5 us

profile of v1, /device:TPU:0, one launch (start us, length us, event | category | flops | bytes accessed | tf_op | source)
XLA Modules:
  0.0 523.8 jit_solution(12593255206809867275)
XLA Ops:
  0.7 173.8 %shard_map.238 = (bf16[4,2,2,64,1024]{4,3,2,1,0:T(8,128)(2,1)}, bf16[4,2,2,64,512]{4,3,2,1,0:T(8,128)(2,1)}, bf16[4,2,2,64,512]{4,3,2,1,0:T(8,128)(2,1)}, bf16[4...) custom-call(bf16[64,1024]{1,0:T(8,128)(2,1)} %refs_0_.1, ...), custom_call_target="tpu_custom_call" | custom-call | tf_op jit(solution)/shard_map/pallas_call | solution.py:242
  174.5 2.3 copy.27
  178.8 3.3 shard_map.237
  186.7 2.6 copy.28
  189.3 2.4 multiply_reduce_fusion.3
  197.8 3.5 fusion.14.in_ref
  201.3 4.0 shard_map.239
  209.1 3.3 shard_map.240
  212.5 4.3 fusion.28
  216.8 2.1 fusion.27
  221.2 3.3 shard_map.242
  224.5 5.6 %multiply_convert_fusion = (bf16[256,1536]{1,0:T(8,128)(2,1)}, bf16[256,1536]{1,0:T(8,128)(2,1)}, bf16[256,1536]{1,0:T(8,128)(2,1)S(1)}) fusion(f32[256,1536]{1,0:T(8,128)} %fusion.27, f32[256,1536]{1,0:T(8,128)} %fusion.28, bf16[256,1024]{1,0:T(8,128)(2,1)} %bitcast.186, bf16[1024,1536]{1,0:T(8,128)(2,1)} %bitcast.212), kind=kOutput, calls=%fused_computation.13 | convolution fusion | flops 811597824 | bytes 9175040 | tf_op jit(solution)/shard_map/dot_general | solution.py:636
  233.0 4.0 shard_map.241
  237.1 3.3 fusion.30
  242.4 4.2 shard_map.243
  248.6 2.7 fusion.25
  251.2 3.3 shard_map.244
  254.5 3.3 convolution_convert_fusion.8
  270.5 4.0 shard_map.245
  277.6 2.6 convolution_convert_fusion.1
  280.3 2.7 convolution_convert_fusion.2
  283.0 2.1 convolution_convert_fusion.3
  290.2 2.7 convolution_convert_fusion
  292.9 221.1 %shard_map.246 = (f32[64,1024]{1,0:T(8,128)}, f32[64,512]{1,0:T(8,128)}, f32[64,512]{1,0:T(8,128)}, f32[64,1024]{1,0:T(8,128)}, f32[64,1536]{1,0:T(8,128)}, /*in...) custom-call(bf16[4,2,2,64,1024]{4,3,2,1,0:T(8,128)(2,1)} %bitcast.168, ...), custom_call_target="tpu_custom_call" | custom-call | tf_op jit(solution)/shard_map/pallas_call | solution.py:450
  (189 shorter events, 55.1 us)
Async XLA Ops:
  0.6 176.1 %copy-start.14 = (bf16[128,1024]{1,0:T(8,128)(2,1)S(1)}, bf16[128,1024]{1,0:T(8,128)(2,1)}, u32[]{:S(2)}) copy-start(bf16[128,1024]{1,0:T(8,128)(2,1)} %param.14) | copy-start | bytes 786436
  0.7 177.3 %copy-start.47 = (f32[1024]{0:T(1024)S(1)}, f32[1024]{0:T(1024)}, u32[]{:S(2)}) copy-start(f32[1024]{0:T(1024)} %param.24) | copy-start | bytes 12292
  176.7 8.1 %copy-start.52 = (f32[128]{0:T(128)S(1)}, f32[128]{0:T(128)}, u32[]{:S(2)}) copy-start(f32[128]{0:T(128)} %param.27) | copy-start | bytes 1540
  182.1 4.6 copy-start.6
  196.8 4.5 copy-start.11
  206.6 5.9 %copy-start.5 = (f32[128,1024]{1,0:T(8,128)}, f32[128,1024]{1,0:T(8,128)S(1)}, u32[]{:S(2)}) copy-start(f32[128,1024]{1,0:T(8,128)S(1)} %get-tuple-element.54) | copy-start | bytes 1572868
  212.4 4.3 copy-start
  212.5 4.3 copy-start.20
  224.5 6.5 %copy-start.61 = (bf16[4,2,2,64,1536]{4,3,2,1,0:T(8,128)(2,1)S(1)}, bf16[4,2,2,64,1536]{4,3,2,1,0:T(8,128)(2,1)}, u32[]{:S(2)}) copy-start(bf16[4,2,2,64,1536]{4,3,2,1,0:T(8,128)(2,1)} %get-tuple-element.34) | copy-start | bytes 9437188
  261.5 6.8 %copy-start.23 = (bf16[4,128,256]{2,1,0:T(8,128)(2,1)}, bf16[4,128,256]{2,1,0:T(8,128)(2,1)S(1)}, u32[]{:S(2)}) copy-start(bf16[4,128,256]{2,1,0:T(8,128)(2,1)S(1)} %fusion.4) | copy-start | bytes 786436
  269.1 5.5 %copy-start.48 = (f32[1024]{0:T(1024)S(1)}, f32[1024]{0:T(1024)}, u32[]{:S(2)}) copy-start(f32[1024]{0:T(1024)} %param.24) | copy-start | bytes 12292
  269.1 5.5 %copy-start.56 = (f32[128]{0:T(128)S(1)}, f32[128]{0:T(128)}, u32[]{:S(2)}) copy-start(f32[128]{0:T(128)} %copy-done.55) | copy-start | bytes 1540
  269.1 6.8 %copy-start.51 = (f32[1024]{0:T(1024)S(1)}, f32[1024]{0:T(1024)}, u32[]{:S(2)}) copy-start(f32[1024]{0:T(1024)} %get-tuple-element.47) | copy-start | bytes 12292
  269.1 8.6 %copy-start.22 = (bf16[256,1536]{1,0:T(8,128)(2,1)S(1)}, bf16[256,1536]{1,0:T(8,128)(2,1)}, u32[]{:S(2)}) copy-start(bf16[256,1536]{1,0:T(8,128)(2,1)} %get-tuple-element.55) | copy-start | bytes 2359300
  286.6 3.6 copy-start.33
  292.9 223.8 %copy-start.15 = (f32[128,1024]{1,0:T(8,128)S(1)}, f32[128,1024]{1,0:T(8,128)}, u32[]{:S(2)}) copy-start(f32[128,1024]{1,0:T(8,128)} %shard_map.245) | copy-start | bytes 1572868
  292.9 223.8 %copy-start.26 = (f32[128,1024]{1,0:T(8,128)S(1)}, f32[128,1024]{1,0:T(8,128)}, u32[]{:S(2)}) copy-start(f32[128,1024]{1,0:T(8,128)} %get-tuple-element.52) | copy-start | bytes 1572868
  292.9 223.8 %copy-start.60 = (f32[128]{0:T(128)S(1)}, f32[128]{0:T(128)}, u32[]{:S(2)}) copy-start(f32[128]{0:T(128)} %get-tuple-element.77) | copy-start | bytes 1540
  514.1 5.4 %copy-start.44 = (f32[64,512]{1,0:T(8,128)S(1)}, f32[64,512]{1,0:T(8,128)}, u32[]{:S(2)}) copy-start(f32[64,512]{1,0:T(8,128)} %get-tuple-element.103) | copy-start | bytes 393220
  514.1 6.1 %copy-start.43 = (f32[64,512]{1,0:T(8,128)S(1)}, f32[64,512]{1,0:T(8,128)}, u32[]{:S(2)}) copy-start(f32[64,512]{1,0:T(8,128)} %get-tuple-element.104) | copy-start | bytes 393220
  514.1 6.7 %copy-start.42 = (f32[64,1024]{1,0:T(8,128)S(1)}, f32[64,1024]{1,0:T(8,128)}, u32[]{:S(2)}) copy-start(f32[64,1024]{1,0:T(8,128)} %get-tuple-element.105) | copy-start | bytes 786436
  514.1 7.4 %copy-start.41 = (f32[64,1536]{1,0:T(8,128)S(1)}, f32[64,1536]{1,0:T(8,128)}, u32[]{:S(2)}) copy-start(f32[64,1536]{1,0:T(8,128)} %get-tuple-element.106) | copy-start | bytes 1179652
  516.8 5.5 %copy-start.40 = (f32[64,1536]{1,0:T(8,128)S(1)}, f32[64,1536]{1,0:T(8,128)}, u32[]{:S(2)}) copy-start(f32[64,1536]{1,0:T(8,128)} %get-tuple-element.107) | copy-start | bytes 1179652
  516.8 6.2 %copy-start.39 = (f32[64,1536]{1,0:T(8,128)S(1)}, f32[64,1536]{1,0:T(8,128)}, u32[]{:S(2)}) copy-start(f32[64,1536]{1,0:T(8,128)} %get-tuple-element.108) | copy-start | bytes 1179652
  (38 other events, 62.4 us)
